TPU v7x, 256 devices: a whole 4x4x8 slice. The times are simulated.
256 devices in a mesh: aux: 16 (over x, z_hi), pair: 16 (over y, z_lo, core).
Axes of the slice: x: 4, y: 4, z: 8 (z_hi: 4, z_lo: 2; z = z_hi * 2 + z_lo), core: 2. Of those that a mesh axis runs over, the one named last changes fastest.
Arguments:
- amplitudes: bfloat16 [512, 36864], P(('aux', 'pair')), may hold values from -6 to 6
- factors: bfloat16 [256, 36864], P('aux'), may hold values from -0.109375 to 0.109375
- sources: int32 [512, 8], P(('aux', 'pair')), may hold values from 0 to 511, as said below
- weights: float32 [512, 8], P(('aux', 'pair')), may hold values from -0.5 to 0.5
- flip_flags: int32 [512, 8], P(('aux', 'pair')), may hold values 0 or 1
Outputs:
- residual: float32 [512, 36864], P(('aux', 'pair'))
Inputs may be any that keep to these rules, and one draw needn't show every extreme that they name: `sources`: every source lies in the same aligned block of 32 pairs as its target pair.
All inputs are finite; a program needn't handle non-finite values. No bound on the sum of `flip_flags` on one device may be relied on, other than what follows from the above.
Results may differ from a plain program's by a relative error of at most 0.0026.
Values may be sent and summed in bfloat16 or wider, within the bound.
No kernel may reach another device: no remote copies, remote signals or barrier semaphores. Data moves between devices by JAX's collectives and lax.ppermute only.
A program may use at most 128 MiB of HBM per device.

v0:
```python
import jax
import jax.numpy as jnp
from jax import lax
from jax.sharding import PartitionSpec as P

V = 192


def ladder_terms(amp_flat, fac_flat):
    virtual = V
    pair_count = amp_flat.shape[0]
    aux_count = fac_flat.shape[0]
    amp_blocks = amp_flat.reshape(pair_count, virtual, virtual)
    fac_blocks = fac_flat.reshape(aux_count, virtual, virtual)
    pair_step = 2
    aux_step = 16
    stacked = fac_blocks.reshape(aux_count // aux_step, aux_step, virtual, virtual)
    grouped = amp_blocks.reshape(pair_count // pair_step, pair_step, virtual, virtual)

    def one_group(members):

        def advance(running, factor_set):
            halfway = jnp.einsum(
                "qab,pbc->pqac", factor_set, members, preferred_element_type=jnp.float32
            ).astype(jnp.bfloat16)
            return (
                running
                + jnp.einsum(
                    "pqac,qdc->pad", halfway, factor_set, preferred_element_type=jnp.float32
                ),
                None,
            )

        initial = jnp.zeros((pair_step, virtual, virtual), jnp.float32)
        result, unused = lax.scan(advance, initial, stacked)
        return result

    return lax.map(one_group, grouped).reshape(pair_count, virtual * virtual)


def local(amplitudes, factors, sources, weights, flip_flags):
    pair_count = amplitudes.shape[0]
    ladder = ladder_terms(amplitudes, lax.all_gather(factors, "aux", axis=0, tiled=True))
    neighbours = lax.all_gather(amplitudes, "pair", axis=0, tiled=True).astype(jnp.float32)
    group_size = neighbours.shape[0]
    local_index = sources % group_size
    onehot = (
        local_index[:, :, None] == jnp.arange(group_size, dtype=jnp.int32)[None, None, :]
    ).astype(jnp.float32)
    flipped = flip_flags.astype(jnp.float32)
    plain_coef = jnp.einsum(
        "pk,pkg->pg", weights * (1.0 - flipped), onehot, precision=lax.Precision.HIGHEST
    )
    turned_coef = jnp.einsum(
        "pk,pkg->pg", weights * flipped, onehot, precision=lax.Precision.HIGHEST
    )
    coupling = jnp.dot(plain_coef, neighbours, precision=lax.Precision.HIGHEST)
    blocks = neighbours.reshape(group_size, V, V)
    turned = jnp.einsum("pg,gca->pac", turned_coef, blocks, precision=lax.Precision.HIGHEST)
    coupling = coupling + turned.reshape(pair_count, V * V)
    return ladder + coupling


def solution(mesh):
    placed = (
        P(("aux", "pair"), None),
        P("aux", None),
        P(("aux", "pair"), None),
        P(("aux", "pair"), None),
        P(("aux", "pair"), None),
    )
    return jax.shard_map(
        local, mesh=mesh, in_specs=placed, out_specs=P(("aux", "pair"), None), check_vma=False
    )
```

profile of v0, /device:TPU:6, one launch (start us, length us, event | category | flops | bytes accessed | tf_op | source)
XLA Modules:
  0.0 396.9 jit_solution(9041273356372757135)
XLA Ops:
  6.5 0.0 all-gather.6.cloned.1.call-start
  6.5 0.7 all-gather.6.cloned.1.call-update
  7.3 0.0 all-gather.4.cloned.1.call-start
  7.3 0.7 all-gather.4.cloned.1.call-update
  8.0 1.8 squeeze.9
  9.8 0.7 and_select_fusion
  10.5 0.7 subtract_multiply_fusion
  11.2 0.2 fusion.33
  11.4 0.2 fusion.34
  11.6 37.3 %all-gather.6.cloned.1.call-done = bf16[16,2,36864]{2,1,0:T(2,128)(2,1)} async-done(((bf16[1,2,36864]{2,1,0:T(2,128)(2,1)}), bf16[16,2,36864]{2,1,0:T(2,128)(2,1)}) %all-gather.6.cloned.1.call-update) | async-done | bytes 2359312 | tf_op jit(solution)/shard_map/all_gather | solution.py:44
  48.9 6.0 %reshape.13 = bf16[32,192,192]{2,1,0:T(8,128)(2,1)S(1)} reshape(bf16[16,2,36864]{2,1,0:T(2,128)(2,1)} %all-gather.6.cloned.1.call-done) | data formatting | bytes 4718592 | tf_op jit(solution)/shard_map/reshape | solution.py:58
  54.9 2.6 fusion.30
  57.5 0.2 copy.10
  57.7 0.3 reshape.14
  58.0 2.9 reshape.16
  60.9 0.0 copy-start
  61.0 0.0 copy-start.1
  61.0 214.3 %all-gather.4.cloned.1.call-done = bf16[256,36864]{1,0:T(8,128)(2,1)} async-done(((bf16[16,36864]{1,0:T(8,128)(2,1)}), bf16[256,36864]{1,0:T(8,128)(2,1)}) %all-gather.4.cloned.1.call-update) | async-done | bytes 18874384 | tf_op jit(solution)/shard_map/all_gather | solution.py:43
  275.3 38.6 %reshape_reshape.4 = bf16[16,16,192,192]{3,2,1,0:T(8,128)(2,1)} reshape(bf16[256,36864]{1,0:T(8,128)(2,1)} %all-gather.4.cloned.1.call-done) | data formatting | bytes 37748736 | tf_op jit(solution)/shard_map/reshape;reshape | solution.py:17
  313.9 0.0 copy-done
  313.9 0.0 copy-done.1
  313.9 74.1 %while.18 = (s32[]{:T(128)}, f32[2,192,192]{2,1,0:T(8,128)S(1)}, bf16[16,16,192,192]{3,2,1,0:T(8,128)(2,1)}, bf16[2,192,192]{2,1,0:T(8,128)(2,1)S(1)}, s32[]{:T(128)}, /*index=5*/s32[]{:T(128)}) while((s32[]{:T(128)}, f32[2,192,192]{2,1,0:T(8,128)S(1)}, bf16[16,16,192,192]{3,2,1,0:T(8,128)(2,1)}, ...), condition=%wide.region_1.2_spmd.clone, body=%wide.region_0.1_spmd.clone.sunk | while | flops 907296768 | bytes 3884630 | solution.py:35
  313.9 4.6 %fusion.52 = f32[2,192,192]{2,1,0:T(8,128)S(1)} fusion(bf16[16,16,192,192]{3,2,1,0:T(8,128)(2,1)} %get-tuple-element.104, s32[]{:T(128)S(6)} %copy.23, f32[2,192,192]{2,1,0:T(8,128)S(1)} %get-tuple-element.97, bf16[2,192,192]{2,1,0:T(8,128)(2,1)S(1)} %get-tuple-element.105, pred[]{:T(512)S(6)} %compare.4), kind=kOutput, calls=%fused_computation.7.clone.1 | convolution fusion | flops 907296768 | bytes 3884544 | tf_op jit(solution)/shard_map/while/body/eval_jaxpr/while/body/eval_jaxpr/pqac,qdc->pad/dot_general | solution.py:28
  318.5 4.6 %fusion.52 = f32[2,192,192]{2,1,0:T(8,128)S(1)} fusion(bf16[16,16,192,192]{3,2,1,0:T(8,128)(2,1)} %get-tuple-element.104, s32[]{:T(128)S(6)} %copy.23, f32[2,192,192]{2,1,0:T(8,128)S(1)} %get-tuple-element.97, bf16[2,192,192]{2,1,0:T(8,128)(2,1)S(1)} %get-tuple-element.105, pred[]{:T(512)S(6)} %compare.4), kind=kOutput, calls=%fused_computation.7.clone.1 | convolution fusion | flops 907296768 | bytes 3884544 | tf_op jit(solution)/shard_map/while/body/eval_jaxpr/while/body/eval_jaxpr/pqac,qdc->pad/dot_general | solution.py:28
  323.1 4.6 %fusion.52 = f32[2,192,192]{2,1,0:T(8,128)S(1)} fusion(bf16[16,16,192,192]{3,2,1,0:T(8,128)(2,1)} %get-tuple-element.104, s32[]{:T(128)S(6)} %copy.23, f32[2,192,192]{2,1,0:T(8,128)S(1)} %get-tuple-element.97, bf16[2,192,192]{2,1,0:T(8,128)(2,1)S(1)} %get-tuple-element.105, pred[]{:T(512)S(6)} %compare.4), kind=kOutput, calls=%fused_computation.7.clone.1 | convolution fusion | flops 907296768 | bytes 3884544 | tf_op jit(solution)/shard_map/while/body/eval_jaxpr/while/body/eval_jaxpr/pqac,qdc->pad/dot_general | solution.py:28
  327.7 4.6 %fusion.52 = f32[2,192,192]{2,1,0:T(8,128)S(1)} fusion(bf16[16,16,192,192]{3,2,1,0:T(8,128)(2,1)} %get-tuple-element.104, s32[]{:T(128)S(6)} %copy.23, f32[2,192,192]{2,1,0:T(8,128)S(1)} %get-tuple-element.97, bf16[2,192,192]{2,1,0:T(8,128)(2,1)S(1)} %get-tuple-element.105, pred[]{:T(512)S(6)} %compare.4), kind=kOutput, calls=%fused_computation.7.clone.1 | convolution fusion | flops 907296768 | bytes 3884544 | tf_op jit(solution)/shard_map/while/body/eval_jaxpr/while/body/eval_jaxpr/pqac,qdc->pad/dot_general | solution.py:28
  332.3 4.6 %fusion.52 = f32[2,192,192]{2,1,0:T(8,128)S(1)} fusion(bf16[16,16,192,192]{3,2,1,0:T(8,128)(2,1)} %get-tuple-element.104, s32[]{:T(128)S(6)} %copy.23, f32[2,192,192]{2,1,0:T(8,128)S(1)} %get-tuple-element.97, bf16[2,192,192]{2,1,0:T(8,128)(2,1)S(1)} %get-tuple-element.105, pred[]{:T(512)S(6)} %compare.4), kind=kOutput, calls=%fused_computation.7.clone.1 | convolution fusion | flops 907296768 | bytes 3884544 | tf_op jit(solution)/shard_map/while/body/eval_jaxpr/while/body/eval_jaxpr/pqac,qdc->pad/dot_general | solution.py:28
  336.9 4.7 %fusion.52 = f32[2,192,192]{2,1,0:T(8,128)S(1)} fusion(bf16[16,16,192,192]{3,2,1,0:T(8,128)(2,1)} %get-tuple-element.104, s32[]{:T(128)S(6)} %copy.23, f32[2,192,192]{2,1,0:T(8,128)S(1)} %get-tuple-element.97, bf16[2,192,192]{2,1,0:T(8,128)(2,1)S(1)} %get-tuple-element.105, pred[]{:T(512)S(6)} %compare.4), kind=kOutput, calls=%fused_computation.7.clone.1 | convolution fusion | flops 907296768 | bytes 3884544 | tf_op jit(solution)/shard_map/while/body/eval_jaxpr/while/body/eval_jaxpr/pqac,qdc->pad/dot_general | solution.py:28
  341.6 4.6 %fusion.52 = f32[2,192,192]{2,1,0:T(8,128)S(1)} fusion(bf16[16,16,192,192]{3,2,1,0:T(8,128)(2,1)} %get-tuple-element.104, s32[]{:T(128)S(6)} %copy.23, f32[2,192,192]{2,1,0:T(8,128)S(1)} %get-tuple-element.97, bf16[2,192,192]{2,1,0:T(8,128)(2,1)S(1)} %get-tuple-element.105, pred[]{:T(512)S(6)} %compare.4), kind=kOutput, calls=%fused_computation.7.clone.1 | convolution fusion | flops 907296768 | bytes 3884544 | tf_op jit(solution)/shard_map/while/body/eval_jaxpr/while/body/eval_jaxpr/pqac,qdc->pad/dot_general | solution.py:28
  346.3 4.7 %fusion.52 = f32[2,192,192]{2,1,0:T(8,128)S(1)} fusion(bf16[16,16,192,192]{3,2,1,0:T(8,128)(2,1)} %get-tuple-element.104, s32[]{:T(128)S(6)} %copy.23, f32[2,192,192]{2,1,0:T(8,128)S(1)} %get-tuple-element.97, bf16[2,192,192]{2,1,0:T(8,128)(2,1)S(1)} %get-tuple-element.105, pred[]{:T(512)S(6)} %compare.4), kind=kOutput, calls=%fused_computation.7.clone.1 | convolution fusion | flops 907296768 | bytes 3884544 | tf_op jit(solution)/shard_map/while/body/eval_jaxpr/while/body/eval_jaxpr/pqac,qdc->pad/dot_general | solution.py:28
  351.0 4.6 %fusion.52 = f32[2,192,192]{2,1,0:T(8,128)S(1)} fusion(bf16[16,16,192,192]{3,2,1,0:T(8,128)(2,1)} %get-tuple-element.104, s32[]{:T(128)S(6)} %copy.23, f32[2,192,192]{2,1,0:T(8,128)S(1)} %get-tuple-element.97, bf16[2,192,192]{2,1,0:T(8,128)(2,1)S(1)} %get-tuple-element.105, pred[]{:T(512)S(6)} %compare.4), kind=kOutput, calls=%fused_computation.7.clone.1 | convolution fusion | flops 907296768 | bytes 3884544 | tf_op jit(solution)/shard_map/while/body/eval_jaxpr/while/body/eval_jaxpr/pqac,qdc->pad/dot_general | solution.py:28
  355.7 4.6 %fusion.52 = f32[2,192,192]{2,1,0:T(8,128)S(1)} fusion(bf16[16,16,192,192]{3,2,1,0:T(8,128)(2,1)} %get-tuple-element.104, s32[]{:T(128)S(6)} %copy.23, f32[2,192,192]{2,1,0:T(8,128)S(1)} %get-tuple-element.97, bf16[2,192,192]{2,1,0:T(8,128)(2,1)S(1)} %get-tuple-element.105, pred[]{:T(512)S(6)} %compare.4), kind=kOutput, calls=%fused_computation.7.clone.1 | convolution fusion | flops 907296768 | bytes 3884544 | tf_op jit(solution)/shard_map/while/body/eval_jaxpr/while/body/eval_jaxpr/pqac,qdc->pad/dot_general | solution.py:28
  360.3 4.6 %fusion.52 = f32[2,192,192]{2,1,0:T(8,128)S(1)} fusion(bf16[16,16,192,192]{3,2,1,0:T(8,128)(2,1)} %get-tuple-element.104, s32[]{:T(128)S(6)} %copy.23, f32[2,192,192]{2,1,0:T(8,128)S(1)} %get-tuple-element.97, bf16[2,192,192]{2,1,0:T(8,128)(2,1)S(1)} %get-tuple-element.105, pred[]{:T(512)S(6)} %compare.4), kind=kOutput, calls=%fused_computation.7.clone.1 | convolution fusion | flops 907296768 | bytes 3884544 | tf_op jit(solution)/shard_map/while/body/eval_jaxpr/while/body/eval_jaxpr/pqac,qdc->pad/dot_general | solution.py:28
  364.9 4.6 %fusion.52 = f32[2,192,192]{2,1,0:T(8,128)S(1)} fusion(bf16[16,16,192,192]{3,2,1,0:T(8,128)(2,1)} %get-tuple-element.104, s32[]{:T(128)S(6)} %copy.23, f32[2,192,192]{2,1,0:T(8,128)S(1)} %get-tuple-element.97, bf16[2,192,192]{2,1,0:T(8,128)(2,1)S(1)} %get-tuple-element.105, pred[]{:T(512)S(6)} %compare.4), kind=kOutput, calls=%fused_computation.7.clone.1 | convolution fusion | flops 907296768 | bytes 3884544 | tf_op jit(solution)/shard_map/while/body/eval_jaxpr/while/body/eval_jaxpr/pqac,qdc->pad/dot_general | solution.py:28
  369.5 4.6 %fusion.52 = f32[2,192,192]{2,1,0:T(8,128)S(1)} fusion(bf16[16,16,192,192]{3,2,1,0:T(8,128)(2,1)} %get-tuple-element.104, s32[]{:T(128)S(6)} %copy.23, f32[2,192,192]{2,1,0:T(8,128)S(1)} %get-tuple-element.97, bf16[2,192,192]{2,1,0:T(8,128)(2,1)S(1)} %get-tuple-element.105, pred[]{:T(512)S(6)} %compare.4), kind=kOutput, calls=%fused_computation.7.clone.1 | convolution fusion | flops 907296768 | bytes 3884544 | tf_op jit(solution)/shard_map/while/body/eval_jaxpr/while/body/eval_jaxpr/pqac,qdc->pad/dot_general | solution.py:28
  374.1 4.6 %fusion.52 = f32[2,192,192]{2,1,0:T(8,128)S(1)} fusion(bf16[16,16,192,192]{3,2,1,0:T(8,128)(2,1)} %get-tuple-element.104, s32[]{:T(128)S(6)} %copy.23, f32[2,192,192]{2,1,0:T(8,128)S(1)} %get-tuple-element.97, bf16[2,192,192]{2,1,0:T(8,128)(2,1)S(1)} %get-tuple-element.105, pred[]{:T(512)S(6)} %compare.4), kind=kOutput, calls=%fused_computation.7.clone.1 | convolution fusion | flops 907296768 | bytes 3884544 | tf_op jit(solution)/shard_map/while/body/eval_jaxpr/while/body/eval_jaxpr/pqac,qdc->pad/dot_general | solution.py:28
  378.7 4.7 %fusion.52 = f32[2,192,192]{2,1,0:T(8,128)S(1)} fusion(bf16[16,16,192,192]{3,2,1,0:T(8,128)(2,1)} %get-tuple-element.104, s32[]{:T(128)S(6)} %copy.23, f32[2,192,192]{2,1,0:T(8,128)S(1)} %get-tuple-element.97, bf16[2,192,192]{2,1,0:T(8,128)(2,1)S(1)} %get-tuple-element.105, pred[]{:T(512)S(6)} %compare.4), kind=kOutput, calls=%fused_computation.7.clone.1 | convolution fusion | flops 907296768 | bytes 3884544 | tf_op jit(solution)/shard_map/while/body/eval_jaxpr/while/body/eval_jaxpr/pqac,qdc->pad/dot_general | solution.py:28
  383.4 4.6 %fusion.52 = f32[2,192,192]{2,1,0:T(8,128)S(1)} fusion(bf16[16,16,192,192]{3,2,1,0:T(8,128)(2,1)} %get-tuple-element.104, s32[]{:T(128)S(6)} %copy.23, f32[2,192,192]{2,1,0:T(8,128)S(1)} %get-tuple-element.97, bf16[2,192,192]{2,1,0:T(8,128)(2,1)S(1)} %get-tuple-element.105, pred[]{:T(512)S(6)} %compare.4), kind=kOutput, calls=%fused_computation.7.clone.1 | convolution fusion | flops 907296768 | bytes 3884544 | tf_op jit(solution)/shard_map/while/body/eval_jaxpr/while/body/eval_jaxpr/pqac,qdc->pad/dot_general | solution.py:28
  388.0 0.3 reshape.12
  388.3 1.8 fusion.27
  (1 shorter events, 0.0 us)
Async XLA Ops:
  6.5 42.3 %all-gather.6.cloned.1.call-start = ((), (), s32[]{:S(2)}) async-start(), calls=%async_computation.1 | async-start | bytes 2506752 | tf_op jit(solution)/shard_map/all_gather | solution.py:44
  7.3 268.1 %all-gather.4.cloned.1.call-start = ((), (), s32[]{:S(2)}) async-start(), calls=%async_computation | async-start | bytes 20054016 | tf_op jit(solution)/shard_map/all_gather | solution.py:43
  60.9 252.9 %copy-start = (f32[2,192,192]{2,1,0:T(8,128)S(1)}, f32[2,192,192]{2,1,0:T(8,128)}, u32[]{:S(2)}) copy-start(f32[2,192,192]{2,1,0:T(8,128)} %custom-call) | copy-start | bytes 884740
  61.0 252.9 %copy-start.1 = (bf16[2,192,192]{2,1,0:T(8,128)(2,1)S(1)}, bf16[2,192,192]{2,1,0:T(8,128)(2,1)}, u32[]{:S(2)}) copy-start(bf16[2,192,192]{2,1,0:T(8,128)(2,1)} %squeeze.9) | copy-start | bytes 442372
Sparse Core Ops, SparseCore 0:
  9.2 39.6 all-gather.5
  51.4 223.9 all-gather.3
where the time goes:
time: 398 us; the launch traced here: 397 us
  waiting for transfers between devices  253 us (64%)
  matrix products  78.5 us (20%)
  local copies, waits for them, and re-layouts  50.1 us (13%)
  between operations  13.5 us (3%)
    all_gather x1, waiting for transfers between devices, local(): lax.all_gather(factors, 'aux', axis=0, tiled=True)  214 us
    dot_general x16, matrix products, advance(): jnp.einsum('pqac,qdc->pad', halfway, factor_set, preferred_element_type=j...  73.7 us
    another operation x1, local copies, waits for them, and re-layouts, ladder_terms(): fac_blocks.reshape(aux_count // aux_step, aux_step, virtual, virtual)  38.6 us
    all_gather x1, waiting for transfers between devices, local(): lax.all_gather(amplitudes, 'pair', axis=0, tiled=True).astype(jnp.float32)  37.3 us
  transfers between devices with their start and end apart: 2, of which 2 were waited for; matrix products, arithmetic and copies ran while one was open for 4% of the time, Pallas kernels for 0%

commit v1 on v0

--- a/solution.py
+++ b/solution.py
@@ -1,9 +1,21 @@
+import functools
 import jax
 import jax.numpy as jnp
 from jax import lax
 from jax.sharding import PartitionSpec as P
 
 V = 192
+
+
+def fix_surface(w_in, device_axis, dimension_no):
+    extra = jnp.concatenate(
+        lax.all_to_all(jnp.stack([w_in] * lax.axis_size(device_axis)), device_axis, 0, 0),
+        axis=dimension_no,
+    )
+    return extra
+
+
+treat_panel_on = functools.partial(fix_surface, device_axis="aux", dimension_no=0)
 
 
 def ladder_terms(amp_flat, fac_flat):
@@ -40,7 +52,7 @@
 
 def local(amplitudes, factors, sources, weights, flip_flags):
     pair_count = amplitudes.shape[0]
-    ladder = ladder_terms(amplitudes, lax.all_gather(factors, "aux", axis=0, tiled=True))
+    ladder = ladder_terms(amplitudes, treat_panel_on(factors))
     neighbours = lax.all_gather(amplitudes, "pair", axis=0, tiled=True).astype(jnp.float32)
     group_size = neighbours.shape[0]
     local_index = sources % group_size

time: 398 us -> 591 us (1.48)
  the two profiles are of different devices: /device:TPU:6 before, /device:TPU:174 now
where the time goes in v1:
time: 591 us; the launch traced here: 590 us
  waiting for transfers between devices  431 us (73%)
  matrix products  78.5 us (13%)
  local copies, waits for them, and re-layouts  56.8 us (10%)
  between operations  13.5 us (2%)
  starting transfers between devices  9.78 us (2%)
    all_to_all x1, waiting for transfers between devices, fix_surface(): lax.all_to_all(jnp.stack([w_in] * lax.axis_size(device_axis)), device_axi...  285 us
    all_gather x1, waiting for transfers between devices, local(): lax.all_gather(amplitudes, 'pair', axis=0, tiled=True).astype(jnp.float32)  145 us
    dot_general x16, matrix products, advance(): jnp.einsum('pqac,qdc->pad', halfway, factor_set, preferred_element_type=j...  73.7 us
    another operation x1, local copies, waits for them, and re-layouts, ladder_terms(): fac_blocks.reshape(aux_count // aux_step, aux_step, virtual, virtual)  38.6 us
  transfers between devices with their start and end apart: 2, of which 2 were waited for; matrix products, arithmetic and copies ran while one was open for 2% of the time, Pallas kernels for 0%

profile of v1, /device:TPU:174, one launch (start us, length us, event | category | flops | bytes accessed | tf_op | source)
XLA Modules:
  0.0 589.7 jit_solution(15852117560583145320)
XLA Ops:
  6.5 7.6 %stack.2 = bf16[16,16,36864]{2,1,0:T(8,128)(2,1)} broadcast(bf16[16,36864]{1,0:T(8,128)(2,1)} %param.8), dimensions={1,2} | broadcast | bytes 20054016 | tf_op jit(solution)/shard_map/stack | solution.py:12
  14.1 0.0 copy-start
  14.1 0.0 copy-start.3
  14.1 0.0 copy-start.4
  14.1 0.0 copy-start.5
  14.1 9.7 %all-to-all-start = ((bf16[16,16,36864]{2,1,0:T(8,128)(2,1)}), bf16[16,16,36864]{2,1,0:T(8,128)(2,1)}, u32[]{:S(2)}, u32[]{:S(2)}) async-start(bf16[16,16,36864]{2,1,0:T(8,128)(2,1)} %stack.2), calls=%async_computation | async-start | bytes 37748736 | tf_op jit(solution)/shard_map/all_to_all | solution.py:12
  23.9 0.0 all-gather.3.cloned.1.call-start
  23.9 0.7 all-gather.3.cloned.1.call-update
  24.6 0.0 copy-done
  24.6 0.9 squeeze.9
  25.5 0.0 copy-done.3
  25.5 0.0 copy-done.4
  25.5 0.0 copy-done.5
  25.6 0.2 fusion.33
  25.8 0.2 fusion.34
  26.0 145.3 %all-gather.3.cloned.1.call-done = bf16[16,2,36864]{2,1,0:T(2,128)(2,1)} async-done(((bf16[1,2,36864]{2,1,0:T(2,128)(2,1)}), bf16[16,2,36864]{2,1,0:T(2,128)(2,1)}) %all-gather.3.cloned.1.call-update) | async-done | bytes 2359312 | tf_op jit(solution)/shard_map/all_gather | solution.py:56
  171.3 6.0 %reshape.15 = bf16[32,192,192]{2,1,0:T(8,128)(2,1)S(1)} reshape(bf16[16,2,36864]{2,1,0:T(2,128)(2,1)} %all-gather.3.cloned.1.call-done) | data formatting | bytes 4718592 | tf_op jit(solution)/shard_map/reshape | solution.py:70
  177.3 2.6 fusion.30
  179.9 0.2 copy.10
  180.1 0.3 reshape.16
  180.4 2.9 reshape.18
  183.3 0.0 copy-start.1
  183.4 0.0 copy-start.2
  183.4 284.8 %all-to-all-done = bf16[16,16,36864]{2,1,0:T(8,128)(2,1)} async-done(((bf16[16,16,36864]{2,1,0:T(8,128)(2,1)}), bf16[16,16,36864]{2,1,0:T(8,128)(2,1)}, u32[]{:S(2)}, u32[]{:S(2)}) %all-to-all-start) | async-done | bytes 18874400 | tf_op jit(solution)/shard_map/all_to_all | solution.py:12
  468.2 38.6 %reshape_reshape_reshape.3 = bf16[16,16,192,192]{3,2,1,0:T(8,128)(2,1)} reshape(bf16[16,16,36864]{2,1,0:T(8,128)(2,1)} %all-to-all-done) | data formatting | bytes 37748736 | tf_op jit(solution)/shard_map/reshape;reshape;reshape | solution.py:29
  506.7 0.0 copy-done.1
  506.7 0.0 copy-done.2
  506.8 74.0 %while.18 = (s32[]{:T(128)}, f32[2,192,192]{2,1,0:T(8,128)S(1)}, bf16[16,16,192,192]{3,2,1,0:T(8,128)(2,1)}, bf16[2,192,192]{2,1,0:T(8,128)(2,1)S(1)}, s32[]{:T(128)}, /*index=5*/s32[]{:T(128)}) while((s32[]{:T(128)}, f32[2,192,192]{2,1,0:T(8,128)S(1)}, bf16[16,16,192,192]{3,2,1,0:T(8,128)(2,1)}, ...), condition=%wide.region_1.2_spmd.clone, body=%wide.region_0.1_spmd.clone.sunk | while | flops 907296768 | bytes 3884630 | solution.py:47
  506.8 4.6 fusion.52
  511.4 4.6 fusion.52
  516.0 4.6 fusion.52
  520.6 4.6 fusion.52
  525.2 4.7 fusion.52
  529.8 4.6 fusion.52
  534.5 4.6 fusion.52
  539.2 4.6 fusion.52
  543.8 4.6 fusion.52
  548.5 4.6 fusion.52
  553.1 4.6 fusion.52
  557.7 4.6 fusion.52
  562.3 4.6 fusion.52
  567.0 4.6 fusion.52
  571.6 4.6 fusion.52
  576.2 4.6 fusion.52
  580.8 0.3 reshape.14
  581.1 1.8 fusion.27
  (3 shorter events, 0.0 us)
Async XLA Ops:
  14.1 10.5 %copy-start = (bf16[2,36864]{1,0:T(2,128)(2,1)S(1)}, bf16[2,36864]{1,0:T(2,128)(2,1)}, u32[]{:S(2)}) copy-start(bf16[2,36864]{1,0:T(2,128)(2,1)} %param.7) | copy-start | bytes 442372
  14.1 11.4 %copy-start.3 = (s32[2,8]{1,0:T(2,128)S(1)}, s32[2,8]{1,0:T(2,128)}, u32[]{:S(2)}) copy-start(s32[2,8]{1,0:T(2,128)} %param.9) | copy-start | bytes 196
  14.1 11.4 %copy-start.4 = (f32[2,8]{1,0:T(2,128)S(1)}, f32[2,8]{1,0:T(2,128)}, u32[]{:S(2)}) copy-start(f32[2,8]{1,0:T(2,128)} %param.10) | copy-start | bytes 196
  14.1 11.4 %copy-start.5 = (s32[2,8]{1,0:T(2,128)S(1)}, s32[2,8]{1,0:T(2,128)}, u32[]{:S(2)}) copy-start(s32[2,8]{1,0:T(2,128)} %param.11) | copy-start | bytes 196
  14.1 454.0 %all-to-all-start = ((bf16[16,16,36864]{2,1,0:T(8,128)(2,1)}), bf16[16,16,36864]{2,1,0:T(8,128)(2,1)}, u32[]{:S(2)}, u32[]{:S(2)}) async-start(bf16[16,16,36864]{2,1,0:T(8,128)(2,1)} %stack.2), calls=%async_computation | async-start | bytes 37748736 | tf_op jit(solution)/shard_map/all_to_all | solution.py:12
  23.9 147.4 %all-gather.3.cloned.1.call-start = ((), (), s32[]{:S(2)}) async-start(), calls=%async_computation.1 | async-start | bytes 2506752 | tf_op jit(solution)/shard_map/all_gather | solution.py:56
  183.3 323.4 %copy-start.1 = (f32[2,192,192]{2,1,0:T(8,128)S(1)}, f32[2,192,192]{2,1,0:T(8,128)}, u32[]{:S(2)}) copy-start(f32[2,192,192]{2,1,0:T(8,128)} %custom-call) | copy-start | bytes 884740
  183.4 323.4 %copy-start.2 = (bf16[2,192,192]{2,1,0:T(8,128)(2,1)S(1)}, bf16[2,192,192]{2,1,0:T(8,128)(2,1)}, u32[]{:S(2)}) copy-start(bf16[2,192,192]{2,1,0:T(8,128)(2,1)} %squeeze.9) | copy-start | bytes 442372
Sparse Core Ops, SparseCore 0:
  26.5 144.6 all-gather.2
